TPU v7x, 32 devices: a whole 2x2x4 slice. The times are simulated.
32 devices in a mesh: band: 4 (over z), lev: 4 (over y, core), grp: 2 (over x).
Axes of the slice: x: 2, y: 2, z: 4, core: 2. Of those that a mesh axis runs over, the one named last changes fastest.
Arguments:
- fourier: bfloat16 [3, 8, 2, 2, 2, 48, 96], P(None, 'lev', None, None, 'grp', 'band'), may hold values from -6 to 6
- legendre: bfloat16 [96, 2, 48, 2, 48], P('band', None, 'lev', 'grp'), may hold values from -0.625 to 0.625
- lat_points: int32 [2, 48], P('grp', 'band'), may hold values from 20 to 400, as said below
- wave_slots: int32 [96], replicated, may hold values from 0 to 95, as said below
- vertical: float32 [8, 8], replicated, may hold values from -2 to 2
Outputs:
- spectral: bfloat16 [96, 2, 4, 8, 2, 48], P('band', None, None, None, None, ('lev', 'grp'))
Inputs may be any that keep to these rules, and one draw needn't show every extreme that they name: `lat_points`: the values are 20 + 4 i for i = 0 .. 95, each once (octahedral point counts of the latitude pairs, spread over devices). `wave_slots`: every wavenumber appears once; slots 2 i and 2 i + 1 hold wavenumbers m and 95 - m.
All inputs are finite; a program needn't handle non-finite values.
Results may differ from a plain program's by a relative error of at most 0.0053.
Values may be sent and summed in bfloat16 or wider, within the bound.
No kernel may reach another device: no remote copies, remote signals or barrier semaphores. Data moves between devices by JAX's collectives and lax.ppermute only.
A program may use at most 64 MiB of HBM per device.

v0:
```python
import jax
import jax.numpy as jnp
from jax import lax
from jax.sharding import PartitionSpec as P


def body(fourier, legendre, lat_points, wave_slots, vertical):
    wave_count = fourier.shape[6]
    cutoff = jnp.minimum(wave_count - 1, (lat_points - 1) // 2)
    wave_ids = lax.broadcasted_iota(jnp.int32, (1, 1, wave_count), 2)
    kept_mask = wave_ids <= cutoff[:, :, None]
    masked = jnp.where(kept_mask, fourier, jnp.zeros((), fourier.dtype))
    slot_table = (
        wave_slots[:, None] == lax.broadcasted_iota(jnp.int32, (wave_count, wave_count), 1)
    ).astype(jnp.bfloat16)
    ordered = lax.dot_general(
        slot_table, masked, (((1,), (6,)), ((), ())), preferred_element_type=jnp.float32
    ).astype(jnp.bfloat16)
    at_owners = lax.all_to_all(ordered, "band", split_axis=0, concat_axis=6, tiled=True)
    coeffs = lax.all_gather(at_owners, "lev", axis=2, tiled=True)
    level_count = coeffs.shape[2]
    level_rows = lax.broadcasted_iota(jnp.int32, (level_count, level_count), 0)
    level_cols = lax.broadcasted_iota(jnp.int32, (level_count, level_count), 1)
    integral = jnp.where(level_cols >= level_rows, vertical, jnp.zeros((), vertical.dtype))
    geopotential = jnp.einsum(
        "lk,skchgr->slchgr",
        integral,
        coeffs[:, 2].astype(jnp.float32),
        precision=lax.Precision.HIGHEST,
    ).astype(jnp.bfloat16)
    fields = jnp.concatenate([coeffs, geopotential[:, None]], axis=1)
    northern = fields[:, :, :, :, 0].astype(jnp.float32)
    southern = fields[:, :, :, :, 1].astype(jnp.float32)
    parity = jnp.stack(
        [(northern + southern).astype(jnp.bfloat16), (northern - southern).astype(jnp.bfloat16)],
        axis=4,
    )
    partial_value = lax.dot_general(
        parity, legendre, (((5, 6), (3, 4)), ((0, 4), (0, 1))), preferred_element_type=jnp.float32
    )
    summed = lax.psum_scatter(partial_value, "grp", scatter_dimension=5, tiled=True)
    slot_count = summed.shape[0]
    half_count = summed.shape[5]
    slot_waves = lax.dynamic_slice_in_dim(
        wave_slots, lax.axis_index("band") * slot_count, slot_count
    )
    block_start = (
        lax.axis_index("lev") * lax.axis_size("grp") + lax.axis_index("grp")
    ) * half_count
    half_ids = block_start + lax.broadcasted_iota(jnp.int32, (1, 1, half_count), 2)
    parity_ids = lax.broadcasted_iota(jnp.int32, (1, 2, 1), 1)
    total = slot_waves[:, None, None] + 2 * half_ids + parity_ids
    valid = (total <= wave_count - 1)[:, :, None, None, None, :]
    return jnp.where(valid, summed, 0.0).astype(jnp.bfloat16)


def solution(mesh):
    placed = (
        P(None, "lev", None, None, "grp", "band", None),
        P("band", None, "lev", "grp", None),
        P("grp", "band"),
        P(),
        P(),
    )
    return jax.shard_map(
        body,
        mesh=mesh,
        in_specs=placed,
        out_specs=P("band", None, None, None, None, ("lev", "grp")),
        check_vma=False,
    )
```

profile of v0, /device:TPU:0, one launch (start us, length us, event | category | flops | bytes accessed | tf_op | source)
XLA Modules:
  0.0 61.3 jit_solution(10844568631659761171)
XLA Ops:
  6.5 0.7 %minimum_bitcast_fusion = s32[12]{0:T(128)S(1)} fusion(s32[1,12]{1,0:T(1,128)} %param.7), kind=kLoop, calls=%fused_computation.34 | loop fusion | flops 204 | bytes 96 | tf_op jit(solution)/shard_map/le | solution.py:11
  7.3 0.1 iota_compare_fusion.1
  7.3 1.0 %fusion.9 = bf16[3,2,2,2,12,96]{5,3,4,2,1,0:T(2,128)(2,1)S(1)} fusion(bf16[3,2,2,2,1,12,96]{6,3,5,4,2,1,0:T(2,128)(2,1)} %param.5, pred[12,96]{1,0:T(8,128)(4,1)S(1)} %iota_compare_fusion.1), kind=kLoop, calls=%fused_computation.19 | loop fusion | flops 27648 | bytes 111744 | tf_op jit(solution)/shard_map/reshape.5
  8.3 0.9 %fusion.1 = bf16[96,3,2,2,2,1,12]{0,6,4,3,2,1,5:T(8,128)(2,1)S(1)} fusion(bf16[3,2,2,2,12,96]{5,3,4,2,1,0:T(2,128)(2,1)S(1)} %fusion.9, s32[96]{0:T(128)} %param.8), kind=kOutput, calls=%fused_computation.3 | convolution fusion | flops 5345280 | bytes 110976 | tf_op jit(solution)/shard_map/dot_general | solution.py:16
  9.2 0.7 %copy.19 = bf16[96,3,2,2,2,1,12]{6,4,3,2,1,5,0:T(2,128)(2,1)S(1)} copy(bf16[96,3,2,2,2,1,12]{0,6,4,3,2,1,5:T(8,128)(2,1)S(1)} %fusion.1) | data formatting | bytes 110592 | tf_op jit(solution)/shard_map/convert_element_type | solution.py:18
  9.8 1.7 %reshape.95 = bf16[4,2,3456]{2,1,0:T(2,128)(2,1)} reshape(bf16[96,1,3,2,2,2,12]{6,5,4,3,2,1,0:T(2,128)(2,1)S(1)} %bitcast.37) | data formatting | bytes 110592
  11.5 6.3 %all-to-all-start = ((bf16[4,2,3456]{2,1,0:T(2,128)(2,1)}), bf16[4,2,3456]{2,1,0:T(2,128)(2,1)S(1)}, u32[]{:S(2)}, u32[]{:S(2)}) async-start(bf16[4,2,3456]{2,1,0:T(2,128)(2,1)} %reshape.95), calls=%async_computation | async-start | bytes 110592 | tf_op jit(solution)/shard_map/all_to_all | solution.py:19
  17.9 0.1 dynamic_slice.3
  17.9 5.6 %all-to-all-done = bf16[4,2,3456]{2,1,0:T(2,128)(2,1)S(1)} async-done(((bf16[4,2,3456]{2,1,0:T(2,128)(2,1)}), bf16[4,2,3456]{2,1,0:T(2,128)(2,1)S(1)}, u32[]{:S(2)}, u32[]{:S(2)}) %all-to-all-start) | async-done | bytes 55328 | tf_op jit(solution)/shard_map/all_to_all | solution.py:19
  23.6 1.4 %reshape.96 = bf16[96,1,3,2,2,2,12]{6,5,4,3,2,1,0:T(2,128)(2,1)S(1)} reshape(bf16[4,2,3456]{2,1,0:T(2,128)(2,1)S(1)} %all-to-all-done) | data formatting | bytes 110592
  25.0 1.0 %copy.32 = bf16[4,24,3,2,2,2,1,12]{1,0,5,7,4,3,2,6:T(4,128)(2,1)S(1)} copy(bf16[4,24,3,2,2,2,1,12]{7,5,4,3,2,1,0,6:T(2,128)(2,1)S(1)} %bitcast.38) | data formatting | bytes 110592 | tf_op jit(solution)/shard_map/all_to_all | solution.py:19
  26.0 0.2 copy.21
  26.2 0.2 copy.22
  26.4 7.6 %all_gather.3 = bf16[24,3,8,2,2,1,48]{6,0,5,4,3,1,2:T(8,128)(2,1)S(1)} all-gather(bf16[24,3,2,2,2,1,48]{6,0,5,4,3,1,2:T(8,128)(2,1)S(1)} %copy.22), channel_id=1, replica_groups=mesh['band'=4,'lev'=4,'grp'=2] {'lev'}, dimensions={2}, use_global_device_ids=true | all-gather | bytes 276480 | tf_op jit(solution)/shard_map/all_gather | solution.py:20
  34.0 0.2 copy_dynamic-update-slice_fusion
  34.2 0.3 fusion
  34.6 0.2 fusion.2
  34.8 0.4 fusion.4
  35.2 2.1 %copy.27 = f32[24,2,4,8,2,12]{0,3,4,2,1,5:T(8,128)} copy(f32[24,2,4,8,2,12]{5,3,4,2,1,0:T(8,128)S(1)} %fusion.4) | data formatting | bytes 294912 | tf_op jit(solution)/shard_map/dot_general | solution.py:38
  37.3 0.0 reduce-scatter.2.cloned.1.call-update
  37.3 0.1 broadcast_add_fusion
  37.4 15.2 %reduce-scatter.2.cloned.1.call-done = f32[24,2,4,8,2,6]{0,3,4,2,1,5:T(8,128)} async-done(((f32[24,2,4,8,2,12]{0,3,4,2,1,5:T(8,128)}), f32[24,2,4,8,2,6]{0,3,4,2,1,5:T(8,128)}) %reduce-scatter.2.cloned.1.call-update) | async-done | bytes 73744 | tf_op jit(solution)/shard_map/reduce_scatter | solution.py:41
  52.6 1.0 %select_convert_fusion = bf16[24,2,4,8,2,6]{0,3,4,2,1,5:T(8,128)(2,1)S(1)} fusion(f32[24,2,4,8,2,6]{0,3,4,2,1,5:T(8,128)} %reduce-scatter.2.cloned.1.call-done, pred[24,2,6]{0,1,2:T(4,128)(4,1)S(1)} %add_compare_fusion), kind=kLoop, calls=%fused_computation.13 | loop fusion | flops 18432 | bytes 110880 | tf_op jit(solution)/shard_map/convert_element_type | solution.py:54
  53.6 0.8 %copy.28 = bf16[24,2,4,8,2,6]{0,4,5,3,2,1:T(2,128)(2,1)} copy(bf16[24,2,4,8,2,6]{0,3,4,2,1,5:T(8,128)(2,1)S(1)} %select_convert_fusion) | data formatting | bytes 73728 | tf_op jit(solution)/shard_map/convert_element_type | solution.py:54
  (11 shorter events, 0.1 us)
Async XLA Ops:
  6.5 28.3 %copy-start = (bf16[24,2,12,1,48]{4,1,3,2,0:T(2,128)(2,1)S(1)}, bf16[24,2,12,1,48]{4,1,3,2,0:T(2,128)(2,1)}, u32[]{:S(2)}) copy-start(bf16[24,2,12,1,48]{4,1,3,2,0:T(2,128)(2,1)} %param.6) | copy-start | bytes 165892
  6.5 11.3 %copy-start.2 = (s32[96]{0:T(128)S(1)}, s32[96]{0:T(128)}, u32[]{:S(2)}) copy-start(s32[96]{0:T(128)} %param.8) | copy-start | bytes 1156
  11.5 12.1 %all-to-all-start = ((bf16[4,2,3456]{2,1,0:T(2,128)(2,1)}), bf16[4,2,3456]{2,1,0:T(2,128)(2,1)S(1)}, u32[]{:S(2)}, u32[]{:S(2)}) async-start(bf16[4,2,3456]{2,1,0:T(2,128)(2,1)} %reshape.95), calls=%async_computation | async-start | bytes 110592 | tf_op jit(solution)/shard_map/all_to_all | solution.py:19
  17.9 34.7 %reduce-scatter.2.cloned.1.call-start = ((), (), s32[]{:S(2)}) async-start(), calls=%async_computation.2 | async-start | bytes 1179648 | tf_op jit(solution)/shard_map/reduce_scatter | solution.py:41
  26.0 8.2 %copy-start.1 = (f32[8,8]{1,0:T(8,128)S(1)}, f32[8,8]{1,0:T(8,128)}, u32[]{:S(2)}) copy-start(f32[8,8]{1,0:T(8,128)} %param.9) | copy-start | bytes 772
Sparse Core Ops, SparseCore 0:
  37.4 15.1 reduce-scatter.1
where the time goes:
time: 61.6 us; the launch traced here: 61.3 us
  waiting for transfers between devices  20.9 us (34%)
  between operations  13.5 us (22%)
  local copies, waits for them, and re-layouts  8.37 us (14%)
  blocking collectives  7.56 us (12%)
  starting transfers between devices  6.35 us (10%)
  other arithmetic  3.09 us (5%)
  matrix products  1.56 us (3%)
    reduce_scatter x1, waiting for transfers between devices, body(): lax.psum_scatter(partial_value, 'grp', scatter_dimension=5, tiled=True)  15.2 us
    all_gather x1, blocking collectives, body(): coeffs = lax.all_gather(at_owners, 'lev', axis=2, tiled=True)  7.56 us
    all_to_all x1, starting transfers between devices, body(): lax.all_to_all(ordered, 'band', split_axis=0, concat_axis=6, tiled=True)  6.35 us
    all_to_all x1, waiting for transfers between devices, body(): lax.all_to_all(ordered, 'band', split_axis=0, concat_axis=6, tiled=True)  5.63 us
    unnamed x9, local copies, waits for them, and re-layouts  3.28 us
    dot_general x1, local copies, waits for them, and re-layouts, body(): lax.dot_general(parity, legendre, (((5, 6), (3, 4)), ((0, 4), (0, 1))), p...  2.07 us
    all_to_all x3, local copies, waits for them, and re-layouts, body(): lax.all_to_all(ordered, 'band', split_axis=0, concat_axis=6, tiled=True)  1.41 us
  transfers between devices with their start and end apart: 2, of which 2 were waited for; matrix products, arithmetic and copies ran while one was open for 0% of the time, Pallas kernels for 0%

commit v1 on v0

--- a/solution.py
+++ b/solution.py
@@ -16,7 +16,19 @@
     ordered = lax.dot_general(
         slot_table, masked, (((1,), (6,)), ((), ())), preferred_element_type=jnp.float32
     ).astype(jnp.bfloat16)
-    at_owners = lax.all_to_all(ordered, "band", split_axis=0, concat_axis=6, tiled=True)
+    ways, here = (lax.axis_size("band"), lax.axis_index("band"))
+    width = ordered.shape[0] // ways
+    shape = list(ordered.shape)
+    shape[0] = width
+    height = shape[6]
+    shape[6] = height * ways
+    full = jnp.zeros(shape, ordered.dtype)
+    for mask in range(ways):
+        part = lax.dynamic_slice_in_dim(ordered, (here ^ mask) * width, width, axis=0)
+        if mask:
+            part = lax.ppermute(part, "band", [(d, d ^ mask) for d in range(ways)])
+        full = lax.dynamic_update_slice_in_dim(full, part, (here ^ mask) * height, axis=6)
+    at_owners = full
     coeffs = lax.all_gather(at_owners, "lev", axis=2, tiled=True)
     level_count = coeffs.shape[2]
     level_rows = lax.broadcasted_iota(jnp.int32, (level_count, level_count), 0)

time: 61.6 us -> 67.2 us (1.091)
  local copies, waits for them, and re-layouts: 8.37 us -> 17.1 us
  waiting for transfers between devices: 20.9 us -> 18 us
    dynamic_update_slice x0 -> x4, local copies, waits for them, and re-layouts: none -> 12.5 us  [body(): lax.dynamic_update_slice_in_dim(full, part, (here ^ mask) * height, axis=6)]
    all_to_all x1 -> x0, starting transfers between devices: 6.35 us -> none  [body(): lax.all_to_all(ordered, 'band', split_axis=0, concat_axis=6, tiled=True)]
    ppermute x0 -> x3, starting transfers between devices: none -> 5.84 us  [body(): part = lax.ppermute(part, 'band', [(d, d ^ mask) for d in range(ways)])]
    all_to_all x1 -> x0, waiting for transfers between devices: 5.63 us -> none  [body(): lax.all_to_all(ordered, 'band', split_axis=0, concat_axis=6, tiled=True)]
    unnamed x9 -> x7, local copies, waits for them, and re-layouts: 3.28 us -> 0.24 us
    reduce_scatter x1, waiting for transfers between devices: 15.2 us -> 17.9 us  [body(): lax.psum_scatter(partial_value, 'grp', scatter_dimension=5, tiled=True)]
    all_to_all x3 -> x0, local copies, waits for them, and re-layouts: 1.41 us -> none  [body(): lax.all_to_all(ordered, 'band', split_axis=0, concat_axis=6, tiled=True)]
    ppermute x0 -> x3, local copies, waits for them, and re-layouts: none -> 0.73 us  [body(): part = lax.ppermute(part, 'band', [(d, d ^ mask) for d in range(ways)])]
  transfers between devices with their start and end apart: 2 -> 4, of which waited for: 2 -> 1; matrix products, arithmetic and copies ran while one was open for 0% -> 14% of each run, Pallas kernels for 0% -> 0%
where the time goes in v1:
time: 67.2 us; the launch traced here: 66.9 us
  waiting for transfers between devices  18 us (27%)
  local copies, waits for them, and re-layouts  17.1 us (25%)
  between operations  13.6 us (20%)
  blocking collectives  7.72 us (11%)
  starting transfers between devices  5.84 us (9%)
  other arithmetic  3.09 us (5%)
  matrix products  1.56 us (2%)
    reduce_scatter x1, waiting for transfers between devices, body(): lax.psum_scatter(partial_value, 'grp', scatter_dimension=5, tiled=True)  17.9 us
    dynamic_update_slice x4, local copies, waits for them, and re-layouts, body(): lax.dynamic_update_slice_in_dim(full, part, (here ^ mask) * height, axis=6)  12.5 us
    all_gather x1, blocking collectives, body(): coeffs = lax.all_gather(at_owners, 'lev', axis=2, tiled=True)  7.72 us
    ppermute x3, starting transfers between devices, body(): part = lax.ppermute(part, 'band', [(d, d ^ mask) for d in range(ways)])  5.84 us
    dot_general x1, local copies, waits for them, and re-layouts, body(): lax.dot_general(parity, legendre, (((5, 6), (3, 4)), ((0, 4), (0, 1))), p...  2.06 us
  transfers between devices with their start and end apart: 4, of which 1 were waited for; matrix products, arithmetic and copies ran while one was open for 14% of the time, Pallas kernels for 0%

profile of v1, /device:TPU:0, one launch (start us, length us, event | category | flops | bytes accessed | tf_op | source)
XLA Modules:
  0.0 66.9 jit_solution(3072772737461175576)
XLA Ops:
  6.5 0.7 %minimum_bitcast_fusion = s32[12]{0:T(128)S(1)} fusion(s32[1,12]{1,0:T(1,128)} %param.7), kind=kLoop, calls=%fused_computation.40 | loop fusion | flops 204 | bytes 96 | tf_op jit(solution)/shard_map/le | solution.py:11
  7.3 1.0 %fusion.8 = bf16[3,2,2,2,12,96]{5,3,4,2,1,0:T(2,128)(2,1)S(1)} fusion(bf16[3,2,2,2,1,12,96]{6,3,5,4,2,1,0:T(2,128)(2,1)} %param.5, pred[12,96]{1,0:T(8,128)(4,1)S(1)} %iota_compare_fusion.1), kind=kLoop, calls=%fused_computation.19 | loop fusion | flops 27648 | bytes 111744 | tf_op jit(solution)/shard_map/reshape.5
  8.3 0.9 %convolution_convert_fusion.1 = bf16[96,3,2,2,2,12]{0,5,4,3,2,1:T(8,128)(2,1)S(1)} fusion(bf16[3,2,2,2,12,96]{5,3,4,2,1,0:T(2,128)(2,1)S(1)} %fusion.8, s32[96]{0:T(128)} %param.8), kind=kOutput, calls=%fused_computation.2 | convolution fusion | flops 5345280 | bytes 110976 | tf_op jit(solution)/shard_map/dot_general | solution.py:16
  9.2 0.2 constant_dynamic-slice_fusion
  9.4 3.1 %collective-permute-start = (bf16[24,3,2,2,2,1,12]{0,4,6,3,2,1,5:T(2,128)(2,1)S(1)}, bf16[24,3,2,2,2,1,12]{0,4,6,3,2,1,5:T(2,128)(2,1)S(1)}, u32[]{:S(2)}, u32[]{:S(2)}) collective-permute-start(bf16[24,3,2,2,2,1,12]{0,4,6,3,2,1,5:T(2,128)(2,1)S(1)} %bitcast.43), channel_id=1, source_target_pairs={{0,8},{8,0},{16,24},{24,16},{1,9},{9,1},{17,25},{25,17},{2,10},{10... | collective-permute-start | bytes 41480 | tf_op jit(solution)/shard_map/ppermute | solution.py:29
  12.6 2.7 %collective-permute-start.1 = (bf16[24,3,2,2,2,1,12]{0,4,6,3,2,1,5:T(2,128)(2,1)S(1)}, bf16[24,3,2,2,2,1,12]{0,4,6,3,2,1,5:T(2,128)(2,1)S(1)}, u32[]{:S(2)}, u32[]{:S(2)}) collective-permute-start(bf16[24,3,2,2,2,1,12]{0,4,6,3,2,1,5:T(2,128)(2,1)S(1)} %bitcast.42), channel_id=1, source_target_pairs={{0,16},{8,24},{16,0},{24,8},{1,17},{9,25},{17,1},{25,9},{2,18},{10... | collective-permute-start | bytes 41480 | tf_op jit(solution)/shard_map/ppermute | solution.py:29
  15.5 0.1 dynamic_slice.15
  15.5 0.2 copy.24
  15.8 0.6 dynamic_update_slice.12
  16.5 0.2 copy.26
  16.7 4.0 %dynamic_update_slice.13 = bf16[24,3,2,2,2,1,48]{6,0,5,4,3,1,2:T(8,128)(2,1)S(1)} dynamic-update-slice(bf16[24,3,2,2,2,1,48]{6,0,5,4,3,1,2:T(8,128)(2,1)S(1)} %dynamic_update_slice.12, bf16[24,3,2,2,2,1,12]{6,0,5,4,3,1,2:T(8,128)(2,1)S(1)} %copy.26, s32[]{:T(128)} %constant.17.clone.1, s32[]{:T(128)} %constant.17.clone.1, s32[]{:T(128)} %constant.17.clone.1, s32[]{:T(128)} %constant.17.clone.1, ...) | dynamic-update-slice | bytes 27652 | tf_op jit(solution)/shard_map/dynamic_update_slice | solution.py:30
  20.7 0.2 copy.28
  20.9 4.0 %dynamic_update_slice.14 = bf16[24,3,2,2,2,1,48]{6,0,5,4,3,1,2:T(8,128)(2,1)S(1)} dynamic-update-slice(bf16[24,3,2,2,2,1,48]{6,0,5,4,3,1,2:T(8,128)(2,1)S(1)} %dynamic_update_slice.13, bf16[24,3,2,2,2,1,12]{6,0,5,4,3,1,2:T(8,128)(2,1)S(1)} %copy.28, s32[]{:T(128)} %constant.17.clone.1, s32[]{:T(128)} %constant.17.clone.1, s32[]{:T(128)} %constant.17.clone.1, s32[]{:T(128)} %constant.17.clone.1, ...) | dynamic-update-slice | bytes 27652 | tf_op jit(solution)/shard_map/dynamic_update_slice | solution.py:30
  24.9 0.2 copy.30
  25.2 4.0 %dynamic_update_slice.15 = bf16[24,3,2,2,2,1,48]{6,0,5,4,3,1,2:T(8,128)(2,1)S(1)} dynamic-update-slice(bf16[24,3,2,2,2,1,48]{6,0,5,4,3,1,2:T(8,128)(2,1)S(1)} %dynamic_update_slice.14, bf16[24,3,2,2,2,1,12]{6,0,5,4,3,1,2:T(8,128)(2,1)S(1)} %copy.30, s32[]{:T(128)} %constant.17.clone.1, s32[]{:T(128)} %constant.17.clone.1, s32[]{:T(128)} %constant.17.clone.1, s32[]{:T(128)} %constant.17.clone.1, ...) | dynamic-update-slice | bytes 27652 | tf_op jit(solution)/shard_map/dynamic_update_slice | solution.py:30
  29.1 7.7 %all_gather.3 = bf16[24,3,8,2,2,1,48]{6,0,5,4,3,1,2:T(8,128)(2,1)S(1)} all-gather(bf16[24,3,2,2,2,1,48]{6,0,5,4,3,1,2:T(8,128)(2,1)S(1)} %dynamic_update_slice.15), channel_id=1, replica_groups=mesh['band'=4,'lev'=4,'grp'=2] {'lev'}, dimensions={2}, use_global_device_ids=true | all-gather | bytes 276480 | tf_op jit(solution)/shard_map/all_gather | solution.py:32
  36.9 0.2 copy_dynamic-update-slice_fusion
  37.1 0.3 fusion
  37.5 0.2 fusion.1
  37.7 0.4 fusion.3
  38.1 2.1 %copy.35 = f32[24,2,4,8,2,12]{0,3,4,2,1,5:T(8,128)} copy(f32[24,2,4,8,2,12]{5,3,4,2,1,0:T(8,128)S(1)} %fusion.3) | data formatting | bytes 294912 | tf_op jit(solution)/shard_map/dot_general | solution.py:50
  40.3 17.9 %reduce-scatter.2.cloned.1.call-done = f32[24,2,4,8,2,6]{0,3,4,2,1,5:T(8,128)} async-done(((f32[24,2,4,8,2,12]{0,3,4,2,1,5:T(8,128)}), f32[24,2,4,8,2,6]{0,3,4,2,1,5:T(8,128)}) %reduce-scatter.2.cloned.1.call-update) | async-done | bytes 73744 | tf_op jit(solution)/shard_map/reduce_scatter | solution.py:53
  58.2 1.0 %select_convert_fusion = bf16[24,2,4,8,2,6]{0,3,4,2,1,5:T(8,128)(2,1)S(1)} fusion(f32[24,2,4,8,2,6]{0,3,4,2,1,5:T(8,128)} %reduce-scatter.2.cloned.1.call-done, pred[24,2,6]{0,1,2:T(4,128)(4,1)S(1)} %add_compare_fusion), kind=kLoop, calls=%fused_computation.12 | loop fusion | flops 18432 | bytes 110880 | tf_op jit(solution)/shard_map/convert_element_type | solution.py:66
  59.3 0.8 %copy.36 = bf16[24,2,4,8,2,6]{0,4,5,3,2,1:T(2,128)(2,1)} copy(bf16[24,2,4,8,2,6]{0,3,4,2,1,5:T(8,128)(2,1)S(1)} %select_convert_fusion) | data formatting | bytes 73728 | tf_op jit(solution)/shard_map/convert_element_type | solution.py:66
  (22 shorter events, 0.5 us)
Async XLA Ops:
  6.5 31.2 %copy-start = (bf16[24,2,12,1,48]{4,1,3,2,0:T(2,128)(2,1)S(1)}, bf16[24,2,12,1,48]{4,1,3,2,0:T(2,128)(2,1)}, u32[]{:S(2)}) copy-start(bf16[24,2,12,1,48]{4,1,3,2,0:T(2,128)(2,1)} %param.6) | copy-start | bytes 165892
  6.5 8.9 %copy-start.2 = (s32[96]{0:T(128)S(1)}, s32[96]{0:T(128)}, u32[]{:S(2)}) copy-start(s32[96]{0:T(128)} %param.8) | copy-start | bytes 1156
  6.5 51.7 %reduce-scatter.2.cloned.1.call-start = ((), (), s32[]{:S(2)}) async-start(), calls=%async_computation.1 | async-start | bytes 1179648 | tf_op jit(solution)/shard_map/reduce_scatter | solution.py:53
  9.4 7.0 %collective-permute-start = (bf16[24,3,2,2,2,1,12]{0,4,6,3,2,1,5:T(2,128)(2,1)S(1)}, bf16[24,3,2,2,2,1,12]{0,4,6,3,2,1,5:T(2,128)(2,1)S(1)}, u32[]{:S(2)}, u32[]{:S(2)}) collective-permute-start(bf16[24,3,2,2,2,1,12]{0,4,6,3,2,1,5:T(2,128)(2,1)S(1)} %bitcast.43), channel_id=1, source_target_pairs={{0,8},{8,0},{16,24},{24,16},{1,9},{9,1},{17,25},{25,17},{2,10},{10... | collective-permute-start | bytes 41480 | tf_op jit(solution)/shard_map/ppermute | solution.py:29
  12.6 8.1 %collective-permute-start.1 = (bf16[24,3,2,2,2,1,12]{0,4,6,3,2,1,5:T(2,128)(2,1)S(1)}, bf16[24,3,2,2,2,1,12]{0,4,6,3,2,1,5:T(2,128)(2,1)S(1)}, u32[]{:S(2)}, u32[]{:S(2)}) collective-permute-start(bf16[24,3,2,2,2,1,12]{0,4,6,3,2,1,5:T(2,128)(2,1)S(1)} %bitcast.42), channel_id=1, source_target_pairs={{0,16},{8,24},{16,0},{24,8},{1,17},{9,25},{17,1},{25,9},{2,18},{10... | collective-permute-start | bytes 41480 | tf_op jit(solution)/shard_map/ppermute | solution.py:29
  15.3 9.6 %collective-permute-start.2 = (bf16[24,3,2,2,2,1,12]{0,4,6,3,2,1,5:T(2,128)(2,1)S(1)}, bf16[24,3,2,2,2,1,12]{0,4,6,3,2,1,5:T(2,128)(2,1)S(1)}, u32[]{:S(2)}, u32[]{:S(2)}) collective-permute-start(bf16[24,3,2,2,2,1,12]{0,4,6,3,2,1,5:T(2,128)(2,1)S(1)} %bitcast.41), channel_id=1, source_target_pairs={{0,24},{8,16},{16,8},{24,0},{1,25},{9,17},{17,9},{25,1},{2,26},{10... | collective-permute-start | bytes 41480 | tf_op jit(solution)/shard_map/ppermute | solution.py:29
  20.9 16.2 %copy-start.1 = (f32[8,8]{1,0:T(8,128)S(1)}, f32[8,8]{1,0:T(8,128)}, u32[]{:S(2)}) copy-start(f32[8,8]{1,0:T(8,128)} %param.9) | copy-start | bytes 772
Sparse Core Ops, SparseCore 0:
  40.3 17.8 reduce-scatter.1
